TPU v7x, 512 devices: a whole 4x8x8 slice. The times are simulated.
512 devices in a mesh: space: 32 (over y, z_lo), mode: 16 (over z_hi, x, core).
Axes of the slice: x: 4, y: 8, z: 8 (z_hi: 2, z_lo: 4; z = z_hi * 4 + z_lo), core: 2. Of those that a mesh axis runs over, the one named last changes fastest.
Arguments:
- left_modes: bfloat16 [2, 12, 4096, 4096], P(None, None, 'space', 'mode'), may hold values from -6 to 6
- right_modes: bfloat16 [32, 2, 12, 4096], P('mode', None, None, 'space'), may hold values from -6 to 6
- momenta: int32 [16, 3], replicated, may hold values from -2 to 2
- coords: int32 [3, 4096], P(None, 'space'), may hold values from 0 to 95
Outputs:
- meson_field: float32 [4096, 16, 2, 32], P(('mode', 'space'))
All inputs are finite; a program needn't handle non-finite values.
Results may differ from a plain program's by a relative error of at most 0.0028.
Values may be sent and summed in bfloat16 or wider, within the bound.
No kernel may reach another device: no remote copies, remote signals or barrier semaphores. Data moves between devices by JAX's collectives and lax.ppermute only.
A program may use at most 64 MiB of HBM per device.

v0:
```python
import math
import jax
import jax.numpy as jnp
from jax import lax
from jax.sharding import PartitionSpec as P

EXTENT = 96


def phase_tables(momenta, coords):
    phase_turns = jnp.mod(jnp.sum(momenta[:, :, None] * coords[None, :, :], axis=1), EXTENT)
    angles = phase_turns.astype(jnp.float32) * (2.0 * math.pi / EXTENT)
    return (jnp.cos(angles), jnp.sin(angles))


def phased_block(right_piece, cosines, sines):
    piece_rows = right_piece.shape[0]
    real_part = right_piece[:, 0].astype(jnp.float32)[None]
    imag_part = right_piece[:, 1].astype(jnp.float32)[None]
    cos_wide = cosines[:, None, None, :]
    sin_wide = sines[:, None, None, :]
    turned_re = (cos_wide * real_part + sin_wide * imag_part).astype(jnp.bfloat16)
    turned_im = (cos_wide * imag_part - sin_wide * real_part).astype(jnp.bfloat16)
    upper_half = jnp.stack([turned_re, turned_im], axis=2)
    lower_half = jnp.stack([turned_im, -turned_re], axis=2)
    stacked = jnp.stack([upper_half, lower_half], axis=1)
    return stacked.reshape(cosines.shape[0] * 2 * piece_rows, -1)


def tile_terms(left_mat, right_piece, cosines, sines):
    stacked = phased_block(right_piece, cosines, sines)
    product = lax.dot_general(
        stacked, left_mat, (((1,), (0,)), ((), ())), preferred_element_type=jnp.float32
    )
    return product.reshape(cosines.shape[0], 2, right_piece.shape[0], left_mat.shape[1])


def body(left_modes, right_modes, momenta, coords):
    cosines, sines = phase_tables(momenta, coords)
    left_mat = left_modes.reshape(-1, left_modes.shape[-1])
    norm_scale = 1.0 / math.sqrt(12 * coords.shape[1] * lax.axis_size("space"))
    partial_value = tile_terms(
        left_mat, lax.all_gather(right_modes, "mode", axis=0, tiled=True), cosines, sines
    )
    owned = lax.psum_scatter(partial_value, "space", scatter_dimension=3, tiled=True)
    summed = jnp.transpose(owned, (3, 0, 1, 2))
    return summed * norm_scale


def solution(mesh):
    in_specs = (
        P(None, None, "space", "mode"),
        P("mode", None, None, "space"),
        P(),
        P(None, "space"),
    )
    out_specs = P(("mode", "space"), None, None, None)
    return jax.shard_map(body, mesh=mesh, in_specs=in_specs, out_specs=out_specs, check_vma=False)
```

profile of v0, /device:TPU:6, one launch (start us, length us, event | category | flops | bytes accessed | tf_op | source)
XLA Modules:
  0.0 231.0 jit_solution(12125679252218744204)
XLA Ops:
  6.5 0.0 copy-start
  6.5 0.0 reduce-scatter.2.cloned.1.call-start
  6.5 0.9 multiply_reduce_fusion
  7.4 0.1 fusion.13
  7.5 27.4 %all_gather.3 = bf16[32,2,12,128]{3,1,2,0:T(2,128)(2,1)S(1)} all-gather(bf16[2,2,12,128]{3,1,2,0:T(2,128)(2,1)} %param.5), channel_id=1, replica_groups=mesh['space'=32,'mode'=16] {'mode'}, dimensions={0}, use_global_device_ids=true | all-gather | bytes 208896 | tf_op jit(solution)/shard_map/all_gather | solution.py:43
  34.9 0.3 fusion.16
  35.2 0.5 fusion.15
  35.7 0.8 add_convert_fusion
  36.6 0.5 maximum_bitcast_fusion
  37.1 0.0 copy-done
  37.1 8.3 %fusion.4 = f32[16,2,32,256]{2,3,1,0:T(8,128)} fusion(bf16[16,1,32,2,12,128]{5,2,4,3,1,0:T(8,128)(2,1)S(1)} %get-tuple-element.6, bf16[16,1,32,2,12,128]{5,2,4,3,1,0:T(8,128)(2,1)S(1)} %get-tuple-element.5, bf16[2,12,128,256]{3,2,1,0:T(8,128)(2,1)S(1)} %copy-done), kind=kOutput, calls=%fused_computation.8 | convolution fusion | flops 1613758464 | bytes 8912896 | tf_op jit(solution)/shard_map/dot_general | solution.py:32
  45.3 0.0 reduce-scatter.2.cloned.1.call-update
  45.4 177.2 %reduce-scatter.2.cloned.1.call-done = f32[16,2,32,8]{2,3,1,0:T(8,128)} async-done(((f32[16,2,32,256]{2,3,1,0:T(8,128)}), f32[16,2,32,8]{2,3,1,0:T(8,128)}) %reduce-scatter.2.cloned.1.call-update) | async-done | bytes 32784 | tf_op jit(solution)/shard_map/reduce_scatter | solution.py:45
  222.6 0.9 multiply_bitcast_fusion
  223.5 0.7 copy.26
  (1 shorter events, 0.0 us)
Async XLA Ops:
  6.5 30.5 %copy-start = (bf16[2,12,128,256]{3,2,1,0:T(8,128)(2,1)S(1)}, bf16[2,12,128,256]{3,2,1,0:T(8,128)(2,1)}, u32[]{:S(2)}) copy-start(bf16[2,12,128,256]{3,2,1,0:T(8,128)(2,1)} %param.4) | copy-start | bytes 4718596
  6.5 216.0 %reduce-scatter.2.cloned.1.call-start = ((), (), s32[]{:S(2)}) async-start(), calls=%async_computation.1 | async-start | bytes 4325376 | tf_op jit(solution)/shard_map/reduce_scatter | solution.py:45
Sparse Core Ops, SparseCore 0:
  45.5 177.0 reduce-scatter.1
where the time goes:
time: 231 us
  waiting for transfers between devices  177 us (77%)
  blocking collectives  27.4 us (12%)
  between operations  13.4 us (6%)
  matrix products  8.26 us (4%)
  other arithmetic  3.73 us (2%)
    reduce_scatter x1, waiting for transfers between devices, body(): lax.psum_scatter(partial_value, 'space', scatter_dimension=3, tiled=True)  177 us
    all_gather x1, blocking collectives, body(): lax.all_gather(right_modes, 'mode', axis=0, tiled=True)  27.4 us
    dot_general x1, matrix products, tile_terms(): lax.dot_general(stacked, left_mat, (((1,), (0,)), ((), ())), preferred_el...  8.26 us
  transfers between devices with their start and end apart: 1, of which 1 were waited for; matrix products, arithmetic and copies ran while one was open for 0% of the time, Pallas kernels for 0%

commit v1 on v0

--- a/solution.py
+++ b/solution.py
@@ -40,7 +40,12 @@
     left_mat = left_modes.reshape(-1, left_modes.shape[-1])
     norm_scale = 1.0 / math.sqrt(12 * coords.shape[1] * lax.axis_size("space"))
     partial_value = tile_terms(
-        left_mat, lax.all_gather(right_modes, "mode", axis=0, tiled=True), cosines, sines
+        left_mat,
+        jnp.concatenate(
+            lax.all_to_all(jnp.stack([right_modes] * lax.axis_size("mode")), "mode", 0, 0), axis=0
+        ),
+        cosines,
+        sines,
     )
     owned = lax.psum_scatter(partial_value, "space", scatter_dimension=3, tiled=True)
     summed = jnp.transpose(owned, (3, 0, 1, 2))

time: 231 us -> 222 us (0.961)
  blocking collectives: 27.4 us -> 0 us
  starting transfers between devices: 0.01 us -> 13.3 us
  waiting for transfers between devices: 177 us -> 181 us
    all_gather x1 -> x0, blocking collectives: 27.4 us -> none  [body(): lax.all_gather(right_modes, 'mode', axis=0, tiled=True)]
    all_to_all x0 -> x1, starting transfers between devices: none -> 13.2 us  [body(): lax.all_to_all(jnp.stack([right_modes] * lax.axis_size('mode')), 'mode',...]
    all_to_all x0 -> x1, waiting for transfers between devices: none -> 8.23 us  [body(): lax.all_to_all(jnp.stack([right_modes] * lax.axis_size('mode')), 'mode',...]
    reduce_scatter x1, waiting for transfers between devices: 177 us -> 172 us  [body(): lax.psum_scatter(partial_value, 'space', scatter_dimension=3, tiled=True)]
  transfers between devices with their start and end apart: 1 -> 2, of which waited for: 1 -> 2; matrix products, arithmetic and copies ran while one was open for 0% -> 0% of each run, Pallas kernels for 0% -> 0%
where the time goes in v1:
time: 222 us
  waiting for transfers between devices  181 us (82%)
  between operations  13.5 us (6%)
  starting transfers between devices  13.3 us (6%)
  matrix products  8.26 us (4%)
  other arithmetic  3.61 us (2%)
  local copies, waits for them, and re-layouts  2.48 us (1%)
    reduce_scatter x1, waiting for transfers between devices, body(): lax.psum_scatter(partial_value, 'space', scatter_dimension=3, tiled=True)  172 us
    all_to_all x1, starting transfers between devices, body(): lax.all_to_all(jnp.stack([right_modes] * lax.axis_size('mode')), 'mode',...  13.2 us
    dot_general x1, matrix products, tile_terms(): lax.dot_general(stacked, left_mat, (((1,), (0,)), ((), ())), preferred_el...  8.26 us
    all_to_all x1, waiting for transfers between devices, body(): lax.all_to_all(jnp.stack([right_modes] * lax.axis_size('mode')), 'mode',...  8.23 us
  transfers between devices with their start and end apart: 2, of which 2 were waited for; matrix products, arithmetic and copies ran while one was open for 0% of the time, Pallas kernels for 0%

profile of v1, /device:TPU:6, one launch (start us, length us, event | category | flops | bytes accessed | tf_op | source)
XLA Modules:
  0.0 221.8 jit_solution(4916182830126353037)
XLA Ops:
  6.5 0.0 copy-start
  6.5 0.8 copy.21
  7.4 0.8 stack.12
  8.2 13.2 %all-to-all-start = ((bf16[16,2,2,12,128]{4,1,3,2,0:T(2,128)(2,1)}), bf16[16,2,2,12,128]{4,1,3,2,0:T(2,128)(2,1)S(1)}, u32[]{:S(2)}, u32[]{:S(2)}) async-start(bf16[16,2,2,12,128]{4,1,3,2,0:T(2,128)(2,1)} %stack.12), calls=%async_computation | async-start | bytes 393216 | tf_op jit(solution)/shard_map/all_to_all | solution.py:45
  21.4 0.0 reduce-scatter.2.cloned.1.call-start
  21.4 0.8 multiply_reduce_fusion
  22.2 0.1 fusion.13
  22.3 8.2 %all-to-all-done = bf16[16,2,2,12,128]{4,1,3,2,0:T(2,128)(2,1)S(1)} async-done(((bf16[16,2,2,12,128]{4,1,3,2,0:T(2,128)(2,1)}), bf16[16,2,2,12,128]{4,1,3,2,0:T(2,128)(2,1)S(1)}, u32[]{:S(2)}, u32[]{:S(2)}) %all-to-all-start) | async-done | bytes 196640 | tf_op jit(solution)/shard_map/all_to_all | solution.py:45
  30.5 0.1 copy.22
  30.7 0.5 fusion.15
  31.2 0.8 add_convert_fusion
  32.0 0.5 maximum_bitcast_fusion
  32.5 0.0 copy-done
  32.6 8.3 %fusion.4 = f32[16,2,32,256]{2,3,1,0:T(8,128)} fusion(bf16[16,1,32,2,12,128]{5,2,4,3,1,0:T(8,128)(2,1)S(1)} %get-tuple-element.6, bf16[16,1,32,2,12,128]{5,2,4,3,1,0:T(8,128)(2,1)S(1)} %get-tuple-element.5, bf16[2,12,128,256]{3,2,1,0:T(8,128)(2,1)S(1)} %copy-done), kind=kOutput, calls=%fused_computation.8 | convolution fusion | flops 1613758464 | bytes 8912896 | tf_op jit(solution)/shard_map/dot_general | solution.py:32
  40.8 0.0 reduce-scatter.2.cloned.1.call-update
  40.8 172.5 %reduce-scatter.2.cloned.1.call-done = f32[16,2,32,8]{2,3,1,0:T(8,128)} async-done(((f32[16,2,32,256]{2,3,1,0:T(8,128)}), f32[16,2,32,8]{2,3,1,0:T(8,128)}) %reduce-scatter.2.cloned.1.call-update) | async-done | bytes 32784 | tf_op jit(solution)/shard_map/reduce_scatter | solution.py:50
  213.3 0.9 multiply_bitcast_fusion
  214.2 0.7 copy.25
  (1 shorter events, 0.0 us)
Async XLA Ops:
  6.5 26.0 %copy-start = (bf16[2,12,128,256]{3,2,1,0:T(8,128)(2,1)S(1)}, bf16[2,12,128,256]{3,2,1,0:T(8,128)(2,1)}, u32[]{:S(2)}) copy-start(bf16[2,12,128,256]{3,2,1,0:T(8,128)(2,1)} %param.4) | copy-start | bytes 4718596
  8.2 22.4 %all-to-all-start = ((bf16[16,2,2,12,128]{4,1,3,2,0:T(2,128)(2,1)}), bf16[16,2,2,12,128]{4,1,3,2,0:T(2,128)(2,1)S(1)}, u32[]{:S(2)}, u32[]{:S(2)}) async-start(bf16[16,2,2,12,128]{4,1,3,2,0:T(2,128)(2,1)} %stack.12), calls=%async_computation | async-start | bytes 393216 | tf_op jit(solution)/shard_map/all_to_all | solution.py:45
  21.4 191.9 %reduce-scatter.2.cloned.1.call-start = ((), (), s32[]{:S(2)}) async-start(), calls=%async_computation.2 | async-start | bytes 4325376 | tf_op jit(solution)/shard_map/reduce_scatter | solution.py:50
Sparse Core Ops, SparseCore 0:
  41.0 172.2 reduce-scatter.1
